TPU v7x, 256 devices: a whole 4x4x8 slice. The times are simulated.
256 devices in a mesh: post: 64 (over x, z, core), rep: 4 (over y).
Axes of the slice: x: 4, y: 4, z: 8, core: 2. Of those that a mesh axis runs over, the one named last changes fastest.
Arguments:
- split_vectors: bfloat16 [2048, 192, 1024], P('post', None, 'rep'), may hold values from -6 to 6
- split_labels: int32 [2048, 192], P('post'), may hold values from 0 to 1, as said below
- split_lengths: int32 [2048], P('post'), may hold values from 144 to 192
- new_owners: int32 [2048, 2], P('post'), may hold values from 0 to 63, all different within a row; in each aligned block of 32 rows (0 to 31, 32 to 63, ...) at most 2 rows name the same one
- neighbour_ids: int32 [2048, 64], replicated, may hold values from 0 to 511, all different within a row
- resident_vectors: bfloat16 [512, 192, 1024], P('post', None, 'rep'), may hold values from -6 to 6
- resident_centroids: bfloat16 [512, 1024], P('post', 'rep'), may hold values from -1 to 1
- resident_lengths: int32 [512], P('post'), may hold values from 1 to 192
Outputs:
- new_postings: bfloat16 [4096, 2, 96, 1024], P('post', None, None, 'rep')
- new_centroids: float32 [2048, 2, 1024], P('post', None, 'rep')
- rescore: float32 [512, 192], P('post')
Inputs may be any that keep to these rules, and one draw needn't show every extreme that they name: `split_labels`: rows at or past a posting's length carry label 1; each half of a split posting holds between 48 and 96 valid rows, and some split has both halves of exactly 96 rows. `new_owners`: the two halves of a split go to different owners; the halves of the splits of one index of post give at most 2 to any one owner. `neighbour_ids`: each split names 64 different postings.
All inputs are finite; a program needn't handle non-finite values.
Results may differ from a plain program's by a relative error of at most 0.0034.
Values may be sent and summed in bfloat16 or wider, within the bound.
No kernel may reach another device: no remote copies, remote signals or barrier semaphores. Data moves between devices by JAX's collectives and lax.ppermute only.
A program may use at most 128 MiB of HBM per device.

v0:
```python
import math
import jax
import jax.numpy as jnp
from jax import lax
from jax.sharding import PartitionSpec as P

D = 1024
far_value = 1e30


def nearest(best_dist, gathered, piece_start, row_data, row_norm, row_onehot, named_table):
    total_cents = gathered.shape[0]
    for block_start in range(0, total_cents, 512):
        block_width = min(512, total_cents - block_start)
        cent_block = gathered[block_start : block_start + block_width]
        cross = lax.dot_general(
            row_data, cent_block, (((1,), (1,)), ((), ())), preferred_element_type=jnp.float32
        )
        block_norm = jnp.einsum(
            "cd,cd->c", cent_block, cent_block, preferred_element_type=jnp.float32
        )
        distance = row_norm[:, None] - 2.0 * cross + block_norm[None, :]
        named_block = lax.dynamic_slice_in_dim(
            named_table, piece_start + block_start, block_width, 1
        )
        row_hits = jnp.dot(row_onehot, named_block, preferred_element_type=jnp.float32)
        distance = jnp.where(row_hits > 0.5, distance, far_value)
        best_dist = jnp.minimum(best_dist, jnp.min(distance, axis=1))
    return best_dist


def body(
    split_vectors,
    split_labels,
    split_lengths,
    new_owners,
    neighbour_ids,
    resident_vectors,
    resident_centroids,
    resident_lengths,
):
    n_post = lax.axis_size("post")
    s_local, length, dim_share = split_vectors.shape
    half_rows = length // 2
    hslot = max(2, 4 * s_local // n_post)
    row_ids = jnp.arange(length)
    is_valid = row_ids[None, :] < split_lengths[:, None]
    in_half = is_valid[:, None, :] & (split_labels[:, None, :] == jnp.arange(2)[None, :, None])
    member_int = in_half.astype(jnp.int32)
    half_rank = jnp.cumsum(member_int, axis=2) - member_int
    placement = in_half[:, :, None, :] & (
        half_rank[:, :, None, :] == jnp.arange(half_rows)[None, None, :, None]
    )
    packed = jnp.einsum(
        "shkr,srd->shkd",
        placement.astype(jnp.bfloat16),
        split_vectors,
        preferred_element_type=jnp.float32,
    ).astype(jnp.bfloat16)
    half_sums = jnp.einsum(
        "shr,srd->shd",
        in_half.astype(jnp.bfloat16),
        split_vectors,
        preferred_element_type=jnp.float32,
    )
    counts = jnp.sum(member_int, axis=2).astype(jnp.float32)
    new_centroids = half_sums / counts[:, :, None]
    owner_flat = new_owners.reshape(-1)
    half_order = jnp.arange(2 * s_local)
    same_owner = (owner_flat[:, None] == owner_flat[None, :]) & (
        half_order[None, :] < half_order[:, None]
    )
    slot_within = jnp.sum(same_owner.astype(jnp.int32), axis=1)
    target_slot = owner_flat * hslot + slot_within
    route_table = (jnp.arange(n_post * hslot)[:, None] == target_slot[None, :]).astype(jnp.bfloat16)
    outgoing = jnp.dot(
        route_table,
        packed.reshape(2 * s_local, half_rows * dim_share),
        preferred_element_type=jnp.float32,
    )
    outgoing = outgoing.astype(jnp.bfloat16).reshape(n_post, hslot, half_rows, dim_share)
    new_postings = lax.all_to_all(outgoing, "post", split_axis=0, concat_axis=0, tiled=True)
    res_local = resident_vectors.shape[0]
    own_diff = (
        resident_vectors.astype(jnp.float32) - resident_centroids.astype(jnp.float32)[:, None, :]
    )
    own_dist = lax.psum(jnp.sum(own_diff * own_diff, axis=2), "rep").reshape(-1)
    post_index = lax.axis_index("post")
    my_postings = post_index * res_local + jnp.arange(res_local)
    hits = jnp.any(neighbour_ids[:, :, None] == my_postings[None, None, :], axis=1)
    named_table = jnp.repeat(hits, 2, axis=0).T.astype(jnp.bfloat16)
    flat_rows = resident_vectors.reshape(res_local * length, dim_share)
    row_data = lax.all_gather(flat_rows, "rep", axis=1, tiled=True)
    row_posting = jnp.arange(res_local * length) // length
    row_norm = jnp.einsum("rd,rd->r", row_data, row_data, preferred_element_type=jnp.float32)
    row_onehot = (row_posting[:, None] == jnp.arange(res_local)[None, :]).astype(jnp.bfloat16)
    centroid_b = new_centroids.astype(jnp.bfloat16).reshape(2 * s_local, dim_share)
    all_shares = lax.all_gather(centroid_b, "post", axis=0, tiled=True)
    all_cents = lax.all_gather(all_shares, "rep", axis=1, tiled=True)
    best_dist = nearest(own_dist, all_cents, 0, row_data, row_norm, row_onehot, named_table)
    scores = (best_dist - row_norm) / math.sqrt(D)
    scores = scores.reshape(res_local, length)
    rescore = jnp.where(row_ids[None, :] < resident_lengths[:, None], scores, 0.0)
    return (new_postings, new_centroids, rescore)


def solution(mesh):
    return jax.shard_map(
        body,
        mesh=mesh,
        in_specs=(
            P("post", None, "rep"),
            P("post", None),
            P("post"),
            P("post", None),
            P(),
            P("post", None, "rep"),
            P("post", "rep"),
            P("post"),
        ),
        out_specs=(P("post", None, None, "rep"), P("post", None, "rep"), P("post", None)),
        check_vma=False,
    )
```

profile of v0, /device:TPU:1, one launch (start us, length us, event | category | flops | bytes accessed | tf_op | source)
XLA Modules:
  0.0 285.8 jit_solution(10616545221353187106)
XLA Ops:
  9.1 1.2 fusion.101
  11.8 1.2 reduce-window.6
  13.4 1.6 fusion.39
  15.0 1.9 copy.83
  17.3 75.5 %all-gather.6.cloned.1.call-done = bf16[4096,256]{1,0:T(8,128)(2,1)} async-done(((bf16[64,256]{1,0:T(8,128)(2,1)}), bf16[4096,256]{1,0:T(8,128)(2,1)}) %all-gather.6.cloned.1.call-update) | async-done | bytes 2097168 | tf_op jit(solution)/shard_map/all_gather | solution.py:98
  92.9 1.8 convolution_convert_fusion
  94.7 4.6 %copy.84 = bf16[16,8,96,256]{3,2,1,0:T(8,128)(2,1)} copy(bf16[16,8,96,256]{3,1,2,0:T(8,128)(2,1)S(1)} %bitcast.85) | data formatting | bytes 12582912
  99.3 7.0 %all-to-all-start = ((bf16[64,2,96,256]{3,2,1,0:T(8,128)(2,1)}), bf16[64,2,96,256]{3,2,1,0:T(8,128)(2,1)}, u32[]{:S(2)}, u32[]{:S(2)}) async-start(bf16[64,2,96,256]{3,2,1,0:T(8,128)(2,1)} %bitcast.84), calls=%async_computation | async-start | bytes 12582912 | tf_op jit(solution)/shard_map/all_to_all | solution.py:82
  107.4 1.0 broadcast_in_dim.15
  108.4 1.3 reshape.111
  110.2 9.5 %psum.7 = f32[1536]{0:T(1024)S(1)} all-reduce(f32[1536]{0:T(1024)S(1)} %reshape.110), channel_id=1, replica_groups=mesh['post'=64,'rep'=4] {'rep'}, use_global_device_ids=true, to_apply=%region_5.6 | all-reduce | flops 1536 | bytes 12288 | tf_op jit(solution)/shard_map/psum | solution.py:87
  119.7 2.4 fusion.75
  122.1 2.3 fusion.74
  124.4 2.3 fusion.73
  126.7 2.3 fusion.72
  129.0 2.4 fusion.71
  131.5 2.4 fusion.70
  133.9 2.4 fusion.69
  136.2 2.3 fusion.68
  138.5 2.7 fusion
  141.3 105.8 %all-to-all-done = bf16[64,2,96,256]{3,2,1,0:T(8,128)(2,1)} async-done(((bf16[64,2,96,256]{3,2,1,0:T(8,128)(2,1)}), bf16[64,2,96,256]{3,2,1,0:T(8,128)(2,1)}, u32[]{:S(2)}, u32[]{:S(2)}) %all-to-all-start) | async-done | bytes 6291488 | tf_op jit(solution)/shard_map/all_to_all | solution.py:82
  247.1 4.4 %fusion.51 = (f32[512]{0:T(512)S(1)}, f32[512]{0:T(512)S(1)}, f32[512]{0:T(512)S(1)}, f32[512]{0:T(512)S(1)}, f32[512]{0:T(512)S(1)}, /*index=5*/f32[512]{0:T(512)S(1)}, f32[512]{0:T(512)S(1)}, f32[512]{0:T(512)S(1)}) fusion(bf16[4096,1024]{1,0:T(8,128)(2,1)} %all-gather.8.cloned.1.call-done), kind=kLoop, calls=%fused_computation.66 | loop fusion | flops 12578816 | bytes 8404992 | tf_op jit(solution)/shard_map/cd,cd->c/dot_general | solution.py:19
  251.5 1.4 copy-done.2
  253.0 4.1 %fusion.52 = f32[1536]{0:T(1024)S(1)} fusion(f32[512]{0:T(512)S(1)} %get-tuple-element.3, bf16[1536,1024]{1,0:T(8,128)(2,1)S(1)} %copy-done.3, f32[1536]{0:T(1024)S(1)} %fusion, f32[1536,512]{0,1:T(8,128)} %fusion.75, bf16[4096,1024]{1,0:T(8,128)(2,1)S(1)} %copy-done.2), kind=kOutput, calls=%fused_computation.68 | convolution fusion | flops 1615329792 | bytes 7356416 | tf_op jit(solution)/shard_map/dot_general | solution.py:16
  257.1 2.1 fusion.53
  259.2 2.1 fusion.54
  261.3 2.1 fusion.55
  263.4 2.1 fusion.56
  265.6 2.1 fusion.57
  267.7 2.3 fusion.58
  270.0 2.1 fusion.59
  272.9 6.5 %copy.93 = bf16[64,2,96,256]{3,2,1,0:T(8,128)(2,1)} copy(bf16[64,2,96,256]{3,2,1,0:T(8,128)(2,1)} %all-to-all-done) | data formatting | bytes 12582912
  (69 shorter events, 6.6 us)
Async XLA Ops:
  7.2 1.9 copy-start
  7.2 85.7 %all-gather.6.cloned.1.call-start = ((), (), s32[]{:S(2)}) async-start(), calls=%async_computation.2 | async-start | bytes 2129920 | tf_op jit(solution)/shard_map/all_gather | solution.py:98
  10.9 127.6 %all-gather.4.cloned.1.call-start = ((), (), s32[]{:S(2)}) async-start(), calls=%async_computation.1 | async-start | bytes 3932160 | tf_op jit(solution)/shard_map/all_gather | solution.py:93
  11.7 235.4 %all-gather.8.cloned.1.call-start = ((), (), s32[]{:S(2)}) async-start(), calls=%async_computation.3 | async-start | bytes 10485760 | tf_op jit(solution)/shard_map/all_gather | solution.py:99
  15.0 2.0 copy-start.14
  99.3 7.0 %copy-start.12 = (s32[2048,64]{0,1:T(8,128)S(1)}, s32[2048,64]{0,1:T(8,128)}, u32[]{:S(2)}) copy-start(s32[2048,64]{0,1:T(8,128)} %param.12) | copy-start | bytes 1572868
  99.3 147.8 %all-to-all-start = ((bf16[64,2,96,256]{3,2,1,0:T(8,128)(2,1)}), bf16[64,2,96,256]{3,2,1,0:T(8,128)(2,1)}, u32[]{:S(2)}, u32[]{:S(2)}) async-start(bf16[64,2,96,256]{3,2,1,0:T(8,128)(2,1)} %bitcast.84), calls=%async_computation | async-start | bytes 12582912 | tf_op jit(solution)/shard_map/all_to_all | solution.py:82
  106.2 3.5 %copy-start.13 = (bf16[8,256]{1,0:T(8,128)(2,1)S(1)}, bf16[8,256]{1,0:T(8,128)(2,1)}, u32[]{:S(2)}) copy-start(bf16[8,256]{1,0:T(8,128)(2,1)} %param.14) | copy-start | bytes 12292
  106.3 3.5 %copy-start.11 = (bf16[8,192,256]{2,1,0:T(8,128)(2,1)S(1)}, bf16[8,192,256]{2,1,0:T(8,128)(2,1)}, u32[]{:S(2)}) copy-start(bf16[8,192,256]{2,1,0:T(8,128)(2,1)} %param.13) | copy-start | bytes 2359300
  138.5 113.0 %copy-start.3 = (bf16[1536,1024]{1,0:T(8,128)(2,1)S(1)}, bf16[1536,1024]{1,0:T(8,128)(2,1)}, u32[]{:S(2)}) copy-start(bf16[1536,1024]{1,0:T(8,128)(2,1)} %all-gather.4.cloned.1.call-done) | copy-start | bytes 9437188
  247.1 5.9 %copy-start.2 = (bf16[4096,1024]{1,0:T(8,128)(2,1)S(1)}, bf16[4096,1024]{1,0:T(8,128)(2,1)}, u32[]{:S(2)}) copy-start(bf16[4096,1024]{1,0:T(8,128)(2,1)} %all-gather.8.cloned.1.call-done) | copy-start | bytes 25165828
  253.0 4.1 %copy-start.10 = (f32[1536,512]{0,1:T(8,128)S(1)}, f32[1536,512]{0,1:T(8,128)}, u32[]{:S(2)}) copy-start(f32[1536,512]{0,1:T(8,128)} %fusion.74) | copy-start | bytes 9437188
  257.1 2.1 copy-start.9
  259.2 2.1 copy-start.8
  261.3 2.1 copy-start.7
  263.4 2.1 copy-start.6
  265.5 2.1 copy-start.5
  267.7 2.3 copy-start.4
  270.0 2.2 copy-start.15
  272.9 6.5 %copy-start.1 = (bf16[32,192,256]{2,1,0:T(8,128)(2,1)S(1)}, bf16[32,192,256]{2,1,0:T(8,128)(2,1)}, u32[]{:S(2)}) copy-start(bf16[32,192,256]{2,1,0:T(8,128)(2,1)} %param.8) | copy-start | bytes 9437188
Sparse Core Ops, SparseCore 0:
  11.4 81.4 all-gather.5
  94.7 42.6 all-gather.3
  139.2 90.3 all-gather.7
where the time goes:
time: 286 us
  waiting for transfers between devices  182 us (64%)
  matrix products  42.2 us (15%)
  local copies, waits for them, and re-layouts  18.6 us (7%)
  between operations  14.2 us (5%)
  other arithmetic  12.2 us (4%)
  blocking collectives  9.52 us (3%)
  starting transfers between devices  7.1 us (2%)
    all_to_all x1, waiting for transfers between devices, body(): lax.all_to_all(outgoing, 'post', split_axis=0, concat_axis=0, tiled=True)  106 us
    all_gather x1, waiting for transfers between devices, body(): all_shares = lax.all_gather(centroid_b, 'post', axis=0, tiled=True)  75.5 us
    dot_general x8, matrix products, nearest(): lax.dot_general(row_data, cent_block, (((1,), (1,)), ((), ())), preferred...  18.9 us
    dot_general x8, matrix products, nearest(): jnp.dot(row_onehot, named_block, preferred_element_type=jnp.float32)  18.8 us
    unnamed x36, local copies, waits for them, and re-layouts  14.6 us
    psum x1, blocking collectives, body(): own_dist = lax.psum(jnp.sum(own_diff * own_diff, axis=2), 'rep').reshape(-1)  9.52 us
    all_to_all x1, starting transfers between devices, body(): lax.all_to_all(outgoing, 'post', split_axis=0, concat_axis=0, tiled=True)  6.98 us
  transfers between devices with their start and end apart: 4, of which 2 were waited for; matrix products, arithmetic and copies ran while one was open for 13% of the time, Pallas kernels for 0%

commit v1 on v0

--- a/solution.py
+++ b/solution.py
@@ -96,7 +96,11 @@
     row_onehot = (row_posting[:, None] == jnp.arange(res_local)[None, :]).astype(jnp.bfloat16)
     centroid_b = new_centroids.astype(jnp.bfloat16).reshape(2 * s_local, dim_share)
     all_shares = lax.all_gather(centroid_b, "post", axis=0, tiled=True)
-    all_cents = lax.all_gather(all_shares, "rep", axis=1, tiled=True)
+    length_2 = lax.axis_size("rep")
+    repeats = [length_2 if d == 1 else 1 for d in range(all_shares.ndim)]
+    all_cents = lax.all_to_all(
+        jnp.tile(all_shares, repeats), "rep", split_axis=1, concat_axis=1, tiled=True
+    )
     best_dist = nearest(own_dist, all_cents, 0, row_data, row_norm, row_onehot, named_table)
     scores = (best_dist - row_norm) / math.sqrt(D)
     scores = scores.reshape(res_local, length)

time: 286 us -> 395 us (1.38); the launches traced: 286 us -> 387 us
  waiting for transfers between devices: 182 us -> 249 us
  local copies, waits for them, and re-layouts: 18.6 us -> 42.1 us
  starting transfers between devices: 7.1 us -> 14.2 us
    all_to_all x0 -> x1, waiting for transfers between devices: none -> 106 us  [body(): lax.all_to_all(jnp.tile(all_shares, repeats), 'rep', split_axis=1, concat...]
    all_to_all x1, waiting for transfers between devices: 106 us -> 60.2 us  [body(): lax.all_to_all(outgoing, 'post', split_axis=0, concat_axis=0, tiled=True)]
    unnamed x36 -> x54, local copies, waits for them, and re-layouts: 14.6 us -> 27.2 us
    all_gather x1, waiting for transfers between devices: 75.5 us -> 82 us  [body(): all_shares = lax.all_gather(centroid_b, 'post', axis=0, tiled=True)]
    all_to_all x0 -> x1, starting transfers between devices: none -> 5.65 us  [body(): lax.all_to_all(jnp.tile(all_shares, repeats), 'rep', split_axis=1, concat...]
    slice x2 -> x3, local copies, waits for them, and re-layouts: 0.18 us -> 5.8 us  [the longest x1 5.61 us: nearest(): cent_block = gathered[block_start:block_start + block_width]]
    another operation x2 -> x3, local copies, waits for them, and re-layouts: 0.01 us -> 5.35 us  [the longest x1 5.34 us: body(): jnp.tile(all_shares, repeats)]
  transfers between devices with their start and end apart: 4 -> 4, of which waited for: 2 -> 3; matrix products, arithmetic and copies ran while one was open for 13% -> 22% of each run, Pallas kernels for 0% -> 0%
where the time goes in v1:
time: 395 us; the launch traced here: 387 us
  waiting for transfers between devices  249 us (63%)
  matrix products  43.4 us (11%)
  local copies, waits for them, and re-layouts  42.1 us (11%)
  between operations  16.2 us (4%)
  starting transfers between devices  14.2 us (4%)
  other arithmetic  14.1 us (4%)
  blocking collectives  7.76 us (2%)
    all_to_all x1, waiting for transfers between devices, body(): lax.all_to_all(jnp.tile(all_shares, repeats), 'rep', split_axis=1, concat...  106 us
    all_gather x1, waiting for transfers between devices, body(): all_shares = lax.all_gather(centroid_b, 'post', axis=0, tiled=True)  82 us
    all_to_all x1, waiting for transfers between devices, body(): lax.all_to_all(outgoing, 'post', split_axis=0, concat_axis=0, tiled=True)  60.2 us
    unnamed x54, local copies, waits for them, and re-layouts  27.2 us
    dot_general x8, matrix products, nearest(): lax.dot_general(row_data, cent_block, (((1,), (1,)), ((), ())), preferred...  20.1 us
    dot_general x8, matrix products, nearest(): jnp.dot(row_onehot, named_block, preferred_element_type=jnp.float32)  18.8 us
    all_to_all x1, starting transfers between devices, body(): lax.all_to_all(outgoing, 'post', split_axis=0, concat_axis=0, tiled=True)  8.44 us
  transfers between devices with their start and end apart: 4, of which 3 were waited for; matrix products, arithmetic and copies ran while one was open for 22% of the time, Pallas kernels for 0%

profile of v1, /device:TPU:1, one launch (start us, length us, event | category | flops | bytes accessed | tf_op | source)
XLA Modules:
  0.0 386.9 jit_solution(8164489738134917232)
XLA Ops:
  11.8 82.0 %all-gather.5.cloned.1.call-done = bf16[4096,256]{1,0:T(8,128)(2,1)} async-done(((bf16[64,256]{1,0:T(8,128)(2,1)}), bf16[4096,256]{1,0:T(8,128)(2,1)}) %all-gather.5.cloned.1.call-update) | async-done | bytes 2097168 | tf_op jit(solution)/shard_map/all_gather | solution.py:98
  93.7 5.3 %tile.2 = bf16[4096,4,256]{2,0,1:T(8,128)(2,1)} broadcast(bf16[4096,256]{1,0:T(8,128)(2,1)} %all-gather.5.cloned.1.call-done), dimensions={0,2} | broadcast | bytes 10485760 | tf_op jit(solution)/shard_map/tile | solution.py:102
  99.1 5.7 %all-to-all-start.1 = ((bf16[4096,4,256]{2,0,1:T(8,128)(2,1)}), bf16[4096,4,256]{2,0,1:T(8,128)(2,1)}, u32[]{:S(2)}, u32[]{:S(2)}) async-start(bf16[4096,4,256]{2,0,1:T(8,128)(2,1)} %tile.2), calls=%async_computation.1 | async-start | bytes 16777216 | tf_op jit(solution)/shard_map/all_to_all | solution.py:101
  112.7 4.6 %copy.118 = bf16[16,8,96,256]{3,2,1,0:T(8,128)(2,1)} copy(bf16[16,8,96,256]{3,1,2,0:T(8,128)(2,1)S(1)} %bitcast.109) | data formatting | bytes 12582912
  117.3 106.4 %all-to-all-done.1 = bf16[4096,4,256]{2,0,1:T(8,128)(2,1)} async-done(((bf16[4096,4,256]{2,0,1:T(8,128)(2,1)}), bf16[4096,4,256]{2,0,1:T(8,128)(2,1)}, u32[]{:S(2)}, u32[]{:S(2)}) %all-to-all-start.1) | async-done | bytes 8388640 | tf_op jit(solution)/shard_map/all_to_all | solution.py:101
  223.7 8.4 %all-to-all-start = ((bf16[64,2,96,256]{3,2,1,0:T(8,128)(2,1)}), bf16[64,2,96,256]{3,2,1,0:T(8,128)(2,1)}, u32[]{:S(2)}, u32[]{:S(2)}) async-start(bf16[64,2,96,256]{3,2,1,0:T(8,128)(2,1)} %bitcast.108), calls=%async_computation | async-start | bytes 12582912 | tf_op jit(solution)/shard_map/all_to_all | solution.py:82
  236.1 7.8 %psum.7 = f32[1536]{0:T(1024)S(1)} all-reduce(f32[1536]{0:T(1024)S(1)} %reshape.125), channel_id=1, replica_groups=mesh['post'=64,'rep'=4] {'rep'}, use_global_device_ids=true, to_apply=%region_5.6 | all-reduce | flops 1536 | bytes 12288 | tf_op jit(solution)/shard_map/psum | solution.py:87
  243.9 2.3 fusion.67
  246.2 2.3 fusion.66
  248.5 2.4 fusion.65
  250.9 2.3 fusion.64
  253.3 2.4 fusion.63
  255.6 2.3 fusion.62
  257.9 2.4 fusion.61
  260.3 2.4 fusion.60
  262.7 2.6 fusion
  265.3 5.6 %fusion.93 = (bf16[512,4,256]{2,0,1:T(8,128)(2,1)}, bf16[512,4,256]{2,0,1:T(8,128)(2,1)S(1)}, bf16[512,4,256]{2,0,1:T(8,128)(2,1)S(1)}, bf16[512,4,256]{2,0,1:T(...) fusion(bf16[4096,4,256]{2,0,1:T(8,128)(2,1)} %all-to-all-done.1), kind=kLoop, calls=%fused_computation.129 | loop fusion | bytes 16777216 | tf_op jit(solution)/shard_map/slice | solution.py:15
  270.9 2.3 copy.107
  273.2 2.3 copy.108
  275.5 2.3 copy.109
  277.7 2.3 copy.110
  280.0 2.3 copy.111
  291.5 4.3 %fusion.52 = f32[1536]{0:T(1024)S(1)} fusion(f32[512]{0:T(512)S(1)} %fusion.51, bf16[512,1024]{0,1:T(8,128)(2,1)S(1)} %bitcast.118, bf16[1536,1024]{1,0:T(8,128)(2,1)S(1)} %copy-done.8, f32[1536]{0:T(1024)S(1)} %fusion, f32[1536,512]{0,1:T(8,128)} %fusion.67), kind=kOutput, calls=%fused_computation.68 | convolution fusion | flops 1615329792 | bytes 7354368 | tf_op jit(solution)/shard_map/dot_general | solution.py:16
  295.8 2.2 fusion.53
  298.1 2.2 fusion.54
  300.4 2.2 fusion.55
  302.6 2.5 fusion.56
  305.1 2.2 fusion.57
  307.3 2.2 fusion.58
  309.6 2.2 fusion.59
  312.6 60.2 %all-to-all-done = bf16[64,2,96,256]{3,2,1,0:T(8,128)(2,1)} async-done(((bf16[64,2,96,256]{3,2,1,0:T(8,128)(2,1)}), bf16[64,2,96,256]{3,2,1,0:T(8,128)(2,1)}, u32[]{:S(2)}, u32[]{:S(2)}) %all-to-all-start) | async-done | bytes 6291488 | tf_op jit(solution)/shard_map/all_to_all | solution.py:82
  372.8 6.5 %copy.127 = bf16[64,2,96,256]{3,2,1,0:T(8,128)(2,1)} copy(bf16[64,2,96,256]{3,2,1,0:T(8,128)(2,1)} %all-to-all-done) | data formatting | bytes 12582912
  (95 shorter events, 25.4 us)
Async XLA Ops:
  8.0 1.9 copy-start
  8.0 85.7 %all-gather.5.cloned.1.call-start = ((), (), s32[]{:S(2)}) async-start(), calls=%async_computation.3 | async-start | bytes 2129920 | tf_op jit(solution)/shard_map/all_gather | solution.py:98
  99.1 124.6 %all-to-all-start.1 = ((bf16[4096,4,256]{2,0,1:T(8,128)(2,1)}), bf16[4096,4,256]{2,0,1:T(8,128)(2,1)}, u32[]{:S(2)}, u32[]{:S(2)}) async-start(bf16[4096,4,256]{2,0,1:T(8,128)(2,1)} %tile.2), calls=%async_computation.1 | async-start | bytes 16777216 | tf_op jit(solution)/shard_map/all_to_all | solution.py:101
  104.7 158.0 %all-gather.3.cloned.1.call-start = ((), (), s32[]{:S(2)}) async-start(), calls=%async_computation.2 | async-start | bytes 3932160 | tf_op jit(solution)/shard_map/all_gather | solution.py:93
  108.6 2.0 copy-start.19
  223.7 8.5 %copy-start.17 = (s32[2048,64]{0,1:T(8,128)S(1)}, s32[2048,64]{0,1:T(8,128)}, u32[]{:S(2)}) copy-start(s32[2048,64]{0,1:T(8,128)} %param.12) | copy-start | bytes 1572868
  223.7 149.1 %all-to-all-start = ((bf16[64,2,96,256]{3,2,1,0:T(8,128)(2,1)}), bf16[64,2,96,256]{3,2,1,0:T(8,128)(2,1)}, u32[]{:S(2)}, u32[]{:S(2)}) async-start(bf16[64,2,96,256]{3,2,1,0:T(8,128)(2,1)} %bitcast.108), calls=%async_computation | async-start | bytes 12582912 | tf_op jit(solution)/shard_map/all_to_all | solution.py:82
  232.1 3.5 copy-start.18
  232.2 3.5 copy-start.16
  284.9 4.8 %copy-start.4 = (bf16[512,4,256]{0,2,1:T(8,128)(2,1)S(1)}, bf16[512,4,256]{0,2,1:T(8,128)(2,1)}, u32[]{:S(2)}) copy-start(bf16[512,4,256]{0,2,1:T(8,128)(2,1)} %copy.110) | copy-start | bytes 3145732
  284.9 5.2 %copy-start.3 = (bf16[512,4,256]{0,2,1:T(8,128)(2,1)S(1)}, bf16[512,4,256]{0,2,1:T(8,128)(2,1)}, u32[]{:S(2)}) copy-start(bf16[512,4,256]{0,2,1:T(8,128)(2,1)} %copy.111) | copy-start | bytes 3145732
  284.9 5.5 %copy-start.2 = (bf16[512,4,256]{0,2,1:T(8,128)(2,1)S(1)}, bf16[512,4,256]{0,2,1:T(8,128)(2,1)}, u32[]{:S(2)}) copy-start(bf16[512,4,256]{0,2,1:T(8,128)(2,1)} %copy.112) | copy-start | bytes 3145732
  288.1 3.4 copy-start.7
  288.1 3.4 copy-start.8
  291.5 4.3 %copy-start.6 = (bf16[512,4,256]{0,2,1:T(8,128)(2,1)S(1)}, bf16[512,4,256]{0,2,1:T(8,128)(2,1)}, u32[]{:S(2)}) copy-start(bf16[512,4,256]{0,2,1:T(8,128)(2,1)} %copy.108) | copy-start | bytes 3145732
  291.5 4.3 %copy-start.15 = (f32[1536,512]{0,1:T(8,128)S(1)}, f32[1536,512]{0,1:T(8,128)}, u32[]{:S(2)}) copy-start(f32[1536,512]{0,1:T(8,128)} %fusion.66) | copy-start | bytes 9437188
  295.8 2.3 copy-start.5
  295.8 2.3 copy-start.14
  298.1 2.2 copy-start.13
  300.3 2.2 copy-start.12
  302.6 2.5 copy-start.11
  305.1 2.2 copy-start.10
  307.3 2.2 copy-start.9
  309.6 2.3 copy-start.20
  372.8 6.5 %copy-start.1 = (bf16[32,192,256]{2,1,0:T(8,128)(2,1)S(1)}, bf16[32,192,256]{2,1,0:T(8,128)(2,1)}, u32[]{:S(2)}) copy-start(bf16[32,192,256]{2,1,0:T(8,128)(2,1)} %param.8) | copy-start | bytes 9437188
Sparse Core Ops, SparseCore 0:
  12.2 81.4 all-gather.4
Sparse Core Ops, SparseCore 1:
  107.0 70.0 all-gather.2
